TPU v7x, 32 devices: a whole 2x2x4 slice. The times are simulated.
32 devices in a mesh: dp: 8 (over z, y), hid: 4 (over x, core).
Axes of the slice: x: 2, y: 2, z: 4, core: 2. Of those that a mesh axis runs over, the one named last changes fastest.
Arguments:
- tokens: bfloat16 [16384, 1024], P('dp', 'hid'), may hold values from -6 to 6
- query_weight: bfloat16 [1024, 1024], P(None, 'hid'), may hold values from -0.1875 to 0.1875
- query_bias: float32 [1024], P('hid'), may hold values from -4 to 4
- key_weight: bfloat16 [1024, 1024], P(None, 'hid'), may hold values from -0.1875 to 0.1875
- value_weight: bfloat16 [1024, 1024], P(None, 'hid'), may hold values from -0.1875 to 0.1875
- value_bias: float32 [1024], P('hid'), may hold values from -4 to 4
- output_weight: bfloat16 [1024, 1024], P('hid'), may hold values from -0.75 to 0.75
- output_bias: float32 [1024], P('hid'), may hold values from -4 to 4
- attention_gain: float32 [1024], P('hid'), may hold values from 0.5 to 1.5
- attention_shift: float32 [1024], P('hid'), may hold values from -4 to 4
- inner_weight: bfloat16 [1024, 4096], P(None, 'hid'), may hold values from -0.1875 to 0.1875
- inner_bias: float32 [4096], P('hid'), may hold values from -4 to 4
- down_weight: bfloat16 [4096, 1024], P('hid'), may hold values from -0.1875 to 0.1875
- down_bias: float32 [1024], P('hid'), may hold values from -4 to 4
- final_gain: float32 [1024], P('hid'), may hold values from 0.5 to 1.5
- final_shift: float32 [1024], P('hid'), may hold values from -4 to 4
- head_alpha: float32 [16], replicated, may hold values from -1 to 3
- unit_alpha: float32 [4096], replicated, may hold values from -1 to 3
- width_alpha: float32 [1024], replicated, may hold values from -1 to 3
- multipliers: float32 [2], replicated, may hold values from -1 to 1
- head_noise: float32 [16], P('hid'), may hold values from 0.02 to 0.98
- unit_noise: float32 [4096], P('hid'), may hold values from 0.02 to 0.98
- width_noise: float32 [1024], P('hid'), may hold values from 0.02 to 0.98
- lengths: int32 [32], replicated, may hold values from 64 to 512, as said below
- teacher: bfloat16 [16384, 1024], P('dp', 'hid'), may hold values from -6 to 6
- upstream: bfloat16 [16384, 1024], P('dp', 'hid'), may hold values from -6 to 6
Outputs:
- output: bfloat16 [16384, 1024], P('dp', 'hid')
- tokens_grad: float32 [16384, 1024], P('dp', 'hid')
- query_weight_grad: float32 [1024, 1024], P(None, 'hid')
- query_bias_grad: float32 [1024], P('hid')
- key_weight_grad: float32 [1024, 1024], P(None, 'hid')
- value_weight_grad: float32 [1024, 1024], P(None, 'hid')
- value_bias_grad: float32 [1024], P('hid')
- output_weight_grad: float32 [1024, 1024], P('hid')
- output_bias_grad: float32 [1024], P('hid')
- attention_gain_grad: float32 [1024], P('hid')
- attention_shift_grad: float32 [1024], P('hid')
- inner_weight_grad: float32 [1024, 4096], P(None, 'hid')
- inner_bias_grad: float32 [4096], P('hid')
- down_weight_grad: float32 [4096, 1024], P('hid')
- down_bias_grad: float32 [1024], P('hid')
- final_gain_grad: float32 [1024], P('hid')
- final_shift_grad: float32 [1024], P('hid')
- head_alpha_grad: float32 [16], P('hid')
- unit_alpha_grad: float32 [4096], P('hid')
- width_alpha_grad: float32 [1024], P('hid')
- distill_mse: float32 [], replicated
- multipliers_new: float32 [2], replicated
Inputs may be any that keep to these rules, and one draw needn't show every extreme that they name: `lengths`: each sequence has 64 to 512 live tokens at its start; in every draw some sequence has 512 and some has 64.
All inputs are finite; a program needn't handle non-finite values.
Results may differ from a plain program's by a relative error of at most 0.02.
Values may be sent and summed in bfloat16 or wider, within the bound.
A program may use at most 192 MiB of HBM per device.

v0:
```python
import jax
import jax.numpy as jnp
from jax import lax
from jax.sharding import PartitionSpec as P

D = 1024
HD = 64
FF = 4096
SLOT = 512
BETA = 2.0 / 3.0
GAMMA = -0.1
ZETA = 1.1
TARGET = 0.7
ASCENT = 1.0
EPS = 1e-12
MASKED = -1000000000.0
ROOT_HALF = 0.7071067811865476
ROOT_TWO_PI = 2.5066282746310002


def erf_gelu(values):
    return 0.5 * values * (1.0 + lax.erf(values * ROOT_HALF))


def gelu_slope(values):
    return (
        0.5 * (1.0 + lax.erf(values * ROOT_HALF))
        + values * jnp.exp(-0.5 * values * values) / ROOT_TWO_PI
    )


def gate_value(noise, alpha):
    logits = (jnp.log(noise) - jnp.log(1.0 - noise) + alpha) / BETA
    stretched = jax.nn.sigmoid(logits) * (ZETA - GAMMA) + GAMMA
    return jnp.clip(stretched, 0.0, 1.0)


def keep_prob(alpha):
    return jax.nn.sigmoid(alpha - BETA * jnp.log(-GAMMA / ZETA))


def lagrangian(head_alpha, unit_alpha, width_alpha, multipliers):
    heads_kept = jnp.sum(keep_prob(head_alpha))
    units_kept = jnp.sum(keep_prob(unit_alpha))
    dims_kept = jnp.sum(keep_prob(width_alpha))
    full_size = 4.0 * D * D + 2.0 * D * FF
    expected = (4.0 * HD * heads_kept * dims_kept + 2.0 * units_kept * dims_kept) / full_size
    gap_value = 1.0 - expected - TARGET
    return multipliers[0] * gap_value + multipliers[1] * gap_value * gap_value


def inner_rows(left_side, right_side):
    return lax.dot_general(
        left_side, right_side, (((0,), (0,)), ((), ())), preferred_element_type=jnp.float32
    )


def times_transpose(left_side, right_side):
    return lax.dot_general(
        left_side, right_side, (((1,), (1,)), ((), ())), preferred_element_type=jnp.float32
    )


def gather_features(sharded):
    return lax.all_gather(sharded, "hid", axis=1, tiled=True)


def branch_total(partial_sum):
    return lax.psum_scatter(
        partial_sum.astype(jnp.bfloat16), "hid", scatter_dimension=1, tiled=True
    ).astype(jnp.float32)


def gather_grads(sharded):
    return lax.all_gather(sharded, "hid", axis=1, tiled=True)


def input_total(partial_sum):
    return lax.psum_scatter(
        partial_sum.astype(jnp.bfloat16), "hid", scatter_dimension=1, tiled=True
    ).astype(jnp.float32)


def norm_forward(residual, scale_gain, shift_bias):
    row_total = lax.psum(jnp.sum(residual, axis=1), "hid")
    row_mean = (row_total / D)[:, None]
    centered = residual - row_mean
    variance = (lax.psum(jnp.sum(centered * centered, axis=1), "hid") / D)[:, None]
    row_rstd = lax.rsqrt(variance + EPS)
    normed = (residual - row_mean) * row_rstd
    return (normed, row_rstd, normed * scale_gain + shift_bias)


def norm_backward(d_output, normed, row_rstd, scale_gain):
    d_normed = d_output * scale_gain
    sum_plain, sum_cross = lax.psum(
        (jnp.sum(d_normed, axis=1), jnp.sum(d_normed * normed, axis=1)), "hid"
    )
    return row_rstd * (d_normed - (sum_plain / D)[:, None] - normed * (sum_cross / D)[:, None])


def on_device(
    tokens,
    query_weight,
    query_bias,
    key_weight,
    value_weight,
    value_bias,
    output_weight,
    output_bias,
    attention_gain,
    attention_shift,
    inner_weight,
    inner_bias,
    down_weight,
    down_bias,
    final_gain,
    final_shift,
    head_alpha,
    unit_alpha,
    width_alpha,
    multipliers,
    head_noise,
    unit_noise,
    width_noise,
    lengths,
    teacher,
    upstream,
):
    row_count, local_width = tokens.shape
    heads_here = local_width // HD
    units_here = inner_weight.shape[1]
    seq_local = row_count // SLOT
    hid_rank = lax.axis_index("hid")
    data_rank = lax.axis_index("dp")
    scale_factor = HD ** (-0.5)
    local_lengths = lax.dynamic_slice_in_dim(lengths, data_rank * seq_local, seq_local)
    key_valid = jnp.arange(SLOT)[None, :] < local_lengths[:, None]
    live_rows = key_valid.reshape(row_count, 1).astype(jnp.float32)
    head_local = lax.dynamic_slice_in_dim(head_alpha, hid_rank * heads_here, heads_here)
    unit_local = lax.dynamic_slice_in_dim(unit_alpha, hid_rank * units_here, units_here)
    width_local = lax.dynamic_slice_in_dim(width_alpha, hid_rank * local_width, local_width)
    head_gate, head_pull = jax.vjp(
        lambda alpha_part: gate_value(head_noise, alpha_part), head_local
    )
    unit_gate, unit_pull = jax.vjp(
        lambda alpha_part: gate_value(unit_noise, alpha_part), unit_local
    )
    width_gate, width_pull = jax.vjp(
        lambda alpha_part: gate_value(width_noise, alpha_part), width_local
    )
    full_tokens = gather_features(tokens)
    shaped = (seq_local, SLOT, heads_here, HD)
    queries = (
        (jnp.dot(full_tokens, query_weight, preferred_element_type=jnp.float32) + query_bias)
        .astype(jnp.bfloat16)
        .reshape(shaped)
    )
    keys_all = (
        jnp.dot(full_tokens, key_weight, preferred_element_type=jnp.float32)
        .astype(jnp.bfloat16)
        .reshape(shaped)
    )
    values = (
        (jnp.dot(full_tokens, value_weight, preferred_element_type=jnp.float32) + value_bias)
        .astype(jnp.bfloat16)
        .reshape(shaped)
    )
    valid_keys = key_valid[:, None, None, :]

    def masked_scores():
        raw_scores = jnp.einsum(
            "sqhd,skhd->shqk", queries, keys_all, preferred_element_type=jnp.float32
        )
        return jnp.where(valid_keys, raw_scores * scale_factor, MASKED)

    scores = masked_scores()
    highest = jnp.max(scores, axis=-1, keepdims=True)
    exponent = jnp.exp(scores - highest)
    totals = jnp.sum(exponent, axis=-1, keepdims=True)
    log_total = highest + jnp.log(totals)
    context = jnp.einsum(
        "shqk,skhd->sqhd",
        (exponent / totals).astype(jnp.bfloat16),
        values,
        preferred_element_type=jnp.float32,
    ).reshape(row_count, heads_here, HD)
    gated_low = (
        (context * head_gate[None, :, None]).reshape(row_count, local_width).astype(jnp.bfloat16)
    )
    attention_pre = (
        branch_total(jnp.dot(gated_low, output_weight, preferred_element_type=jnp.float32))
        + output_bias
    )
    tokens_float = tokens.astype(jnp.float32)
    normed_one, rstd_one, middle = norm_forward(
        tokens_float + attention_pre * width_gate, attention_gain, attention_shift
    )
    middle_low = middle.astype(jnp.bfloat16)
    middle_full = gather_features(middle_low)
    pre_act = jnp.dot(middle_full, inner_weight, preferred_element_type=jnp.float32) + inner_bias
    activated = erf_gelu(pre_act)
    inner_act = (activated * unit_gate).astype(jnp.bfloat16)
    ffn_pre = (
        branch_total(jnp.dot(inner_act, down_weight, preferred_element_type=jnp.float32))
        + down_bias
    )
    normed_two, rstd_two, final_out = norm_forward(
        middle + ffn_pre * width_gate, final_gain, final_shift
    )
    differ = final_out - teacher.astype(jnp.float32)
    squared = lax.psum(jnp.sum(live_rows * differ * differ), ("dp", "hid"))
    distill_mse = squared / (jnp.sum(lengths).astype(jnp.float32) * D)
    d_final = live_rows * (upstream.astype(jnp.float32) + differ)
    final_gain_grad = jnp.sum(d_final * normed_two, axis=0)
    final_shift_grad = jnp.sum(d_final, axis=0)
    d_resid_two = norm_backward(d_final, normed_two, rstd_two, final_gain)
    width_grad = jnp.sum(d_resid_two * ffn_pre, axis=0)
    d_ffn_pre = d_resid_two * width_gate
    down_bias_grad = jnp.sum(d_ffn_pre, axis=0)
    d_ffn_full = gather_grads(d_ffn_pre.astype(jnp.bfloat16))
    down_weight_grad = inner_rows(inner_act, d_ffn_full)
    d_inner = times_transpose(d_ffn_full, down_weight)
    unit_grad = jnp.sum(d_inner * activated, axis=0)
    d_pre = (d_inner * unit_gate * gelu_slope(pre_act)).astype(jnp.bfloat16)
    inner_bias_grad = jnp.sum(d_pre.astype(jnp.float32), axis=0)
    inner_weight_grad = inner_rows(middle_full, d_pre)
    unit_alpha_task = unit_pull(unit_grad)[0]
    d_middle = d_resid_two + input_total(times_transpose(d_pre, inner_weight))
    attention_gain_grad = jnp.sum(d_middle * normed_one, axis=0)
    attention_shift_grad = jnp.sum(d_middle, axis=0)
    d_resid_one = norm_backward(d_middle, normed_one, rstd_one, attention_gain)
    width_grad = width_grad + jnp.sum(d_resid_one * attention_pre, axis=0)
    d_attn_pre = d_resid_one * width_gate
    output_bias_grad = jnp.sum(d_attn_pre, axis=0)
    d_attn_full = gather_grads(d_attn_pre.astype(jnp.bfloat16))
    output_weight_grad = inner_rows(gated_low, d_attn_full)
    d_gated = times_transpose(d_attn_full, output_weight).reshape(row_count, heads_here, HD)
    head_grad = jnp.sum(d_gated * context, axis=(0, 2))
    d_context = (d_gated * head_gate[None, :, None]).astype(jnp.bfloat16).reshape(shaped)
    d_probs = jnp.einsum("sqhd,skhd->shqk", d_context, values, preferred_element_type=jnp.float32)
    probabilities = jnp.exp(masked_scores() - log_total)
    d_scores = (
        probabilities * (d_probs - jnp.sum(probabilities * d_probs, axis=-1, keepdims=True))
    ).astype(jnp.bfloat16)
    d_queries = (
        (
            jnp.einsum("shqk,skhd->sqhd", d_scores, keys_all, preferred_element_type=jnp.float32)
            * scale_factor
        )
        .astype(jnp.bfloat16)
        .reshape(row_count, local_width)
    )
    d_keys = (
        (
            jnp.einsum("shqk,sqhd->skhd", d_scores, queries, preferred_element_type=jnp.float32)
            * scale_factor
        )
        .astype(jnp.bfloat16)
        .reshape(row_count, local_width)
    )
    d_values = (
        jnp.einsum(
            "shqk,sqhd->skhd",
            probabilities.astype(jnp.bfloat16),
            d_context,
            preferred_element_type=jnp.float32,
        )
        .astype(jnp.bfloat16)
        .reshape(row_count, local_width)
    )
    query_bias_grad = jnp.sum(d_queries.astype(jnp.float32), axis=0)
    value_bias_grad = jnp.sum(d_values.astype(jnp.float32), axis=0)
    query_weight_grad = inner_rows(full_tokens, d_queries)
    key_weight_grad = inner_rows(full_tokens, d_keys)
    value_weight_grad = inner_rows(full_tokens, d_values)
    d_tokens_part = (
        times_transpose(d_queries, query_weight)
        + times_transpose(d_keys, key_weight)
        + times_transpose(d_values, value_weight)
    )
    tokens_grad = d_resid_one + input_total(d_tokens_part)
    head_alpha_task = head_pull(head_grad)[0]
    width_alpha_task = width_pull(width_grad)[0]
    (
        query_weight_grad,
        query_bias_grad,
        key_weight_grad,
        value_weight_grad,
        value_bias_grad,
        output_weight_grad,
        output_bias_grad,
        attention_gain_grad,
        attention_shift_grad,
        inner_weight_grad,
        inner_bias_grad,
        down_weight_grad,
        down_bias_grad,
        final_gain_grad,
        final_shift_grad,
        head_alpha_task,
        unit_alpha_task,
        width_alpha_task,
    ) = (
        lax.psum(query_weight_grad.astype(jnp.bfloat16), "dp").astype(jnp.float32),
        lax.psum(query_bias_grad.astype(jnp.bfloat16), "dp").astype(jnp.float32),
        lax.psum(key_weight_grad.astype(jnp.bfloat16), "dp").astype(jnp.float32),
        lax.psum(value_weight_grad.astype(jnp.bfloat16), "dp").astype(jnp.float32),
        lax.psum(value_bias_grad.astype(jnp.bfloat16), "dp").astype(jnp.float32),
        lax.psum(output_weight_grad.astype(jnp.bfloat16), "dp").astype(jnp.float32),
        lax.psum(output_bias_grad.astype(jnp.bfloat16), "dp").astype(jnp.float32),
        lax.psum(attention_gain_grad.astype(jnp.bfloat16), "dp").astype(jnp.float32),
        lax.psum(attention_shift_grad.astype(jnp.bfloat16), "dp").astype(jnp.float32),
        lax.psum(inner_weight_grad.astype(jnp.bfloat16), "dp").astype(jnp.float32),
        lax.psum(inner_bias_grad.astype(jnp.bfloat16), "dp").astype(jnp.float32),
        lax.psum(down_weight_grad.astype(jnp.bfloat16), "dp").astype(jnp.float32),
        lax.psum(down_bias_grad.astype(jnp.bfloat16), "dp").astype(jnp.float32),
        lax.psum(final_gain_grad.astype(jnp.bfloat16), "dp").astype(jnp.float32),
        lax.psum(final_shift_grad.astype(jnp.bfloat16), "dp").astype(jnp.float32),
        lax.psum(head_alpha_task.astype(jnp.bfloat16), "dp").astype(jnp.float32),
        lax.psum(unit_alpha_task.astype(jnp.bfloat16), "dp").astype(jnp.float32),
        lax.psum(width_alpha_task.astype(jnp.bfloat16), "dp").astype(jnp.float32),
    )
    lag_grads = jax.grad(lagrangian, argnums=(0, 1, 2, 3))(
        head_alpha, unit_alpha, width_alpha, multipliers
    )
    head_alpha_grad = head_alpha_task + lax.dynamic_slice_in_dim(
        lag_grads[0], hid_rank * heads_here, heads_here
    )
    unit_alpha_grad = unit_alpha_task + lax.dynamic_slice_in_dim(
        lag_grads[1], hid_rank * units_here, units_here
    )
    width_alpha_grad = width_alpha_task + lax.dynamic_slice_in_dim(
        lag_grads[2], hid_rank * local_width, local_width
    )
    multipliers_new = multipliers + ASCENT * lag_grads[3]
    return (
        final_out.astype(jnp.bfloat16),
        tokens_grad,
        query_weight_grad,
        query_bias_grad,
        key_weight_grad,
        value_weight_grad,
        value_bias_grad,
        output_weight_grad,
        output_bias_grad,
        attention_gain_grad,
        attention_shift_grad,
        inner_weight_grad,
        inner_bias_grad,
        down_weight_grad,
        down_bias_grad,
        final_gain_grad,
        final_shift_grad,
        head_alpha_grad,
        unit_alpha_grad,
        width_alpha_grad,
        distill_mse,
        multipliers_new,
    )


def solution(mesh):
    return jax.shard_map(
        on_device,
        mesh=mesh,
        in_specs=(
            P("dp", "hid"),
            P(None, "hid"),
            P("hid"),
            P(None, "hid"),
            P(None, "hid"),
            P("hid"),
            P("hid", None),
            P("hid"),
            P("hid"),
            P("hid"),
            P(None, "hid"),
            P("hid"),
            P("hid", None),
            P("hid"),
            P("hid"),
            P("hid"),
            P(),
            P(),
            P(),
            P(),
            P("hid"),
            P("hid"),
            P("hid"),
            P(),
            P("dp", "hid"),
            P("dp", "hid"),
        ),
        out_specs=(
            P("dp", "hid"),
            P("dp", "hid"),
            P(None, "hid"),
            P("hid"),
            P(None, "hid"),
            P(None, "hid"),
            P("hid"),
            P("hid", None),
            P("hid"),
            P("hid"),
            P("hid"),
            P(None, "hid"),
            P("hid"),
            P("hid", None),
            P("hid"),
            P("hid"),
            P("hid"),
            P("hid"),
            P("hid"),
            P("hid"),
            P(),
            P(),
        ),
        check_vma=False,
    )
```

profile of v0, /device:TPU:0, one launch (start us, length us, event | category | flops | bytes accessed | tf_op | source)
XLA Modules:
  0.0 802.9 jit_solution(3298500553793230705)
XLA Ops:
  10.2 37.1 %all-gather.5.cloned.1.call-done = bf16[2048,1024]{1,0:T(8,128)(2,1)} async-done(((bf16[2048,256]{1,0:T(8,128)(2,1)}), bf16[2048,1024]{1,0:T(8,128)(2,1)}) %all-gather.5.cloned.1.call-update) | async-done | bytes 4194320 | tf_op jit(solution)/shard_map/all_gather | solution.py:65
  47.3 3.6 convolution_convert_fusion.3
  52.7 4.0 copy.114
  56.7 3.6 fusion.13
  62.1 2.9 copy.113
  65.1 4.9 fusion.12
  70.0 4.4 reshape.158
  74.4 4.0 copy.115
  78.4 8.6 %fusion.60 = (f32[4,4,512]{2,1,0:T(4,128)S(1)}, f32[4,4,512,512]{2,3,1,0:T(8,128)}) fusion(bf16[4,512,4,64]{1,3,2,0:T(8,128)(2,1)S(1)} %copy.113, bf16[4,512,4,64]{1,3,2,0:T(8,128)(2,1)} %copy.114, pred[4,512]{1,0:T(4,128)(4,1)S(1)} %get-tuple-element.162), kind=kOutput, calls=%fused_computation.150 | convolution fusion | flops 549445632 | bytes 18909184 | tf_op jit(solution)/shard_map/sqhd,skhd->shqk/dot_general | solution.py:172
  87.0 8.3 %fusion = f32[4,4,512]{2,1,0:T(4,128)S(1)} fusion(f32[4,4,512,512]{2,3,1,0:T(8,128)} %get-tuple-element.165, f32[4,4,512]{2,1,0:T(4,128)S(1)} %get-tuple-element.164), kind=kLoop, calls=%fused_computation.6 | loop fusion | flops 8380416 | bytes 16842752 | tf_op jit(solution)/shard_map/reduce_sum | solution.py:180
  95.3 7.6 fusion.17
  106.5 3.4 convolution_convert_fusion
  111.9 42.6 %reduce-scatter.5.cloned.1.call-done = bf16[2048,256]{1,0:T(8,128)(2,1)} async-done(((bf16[2048,1024]{1,0:T(8,128)(2,1)}), bf16[2048,256]{1,0:T(8,128)(2,1)}) %reduce-scatter.5.cloned.1.call-update) | async-done | bytes 1048592 | tf_op jit(solution)/shard_map/reduce_scatter | solution.py:69
  156.3 5.9 psum.189
  164.2 5.8 psum.190
  172.7 35.8 %all-gather.7.cloned.1.call-done = bf16[2048,1024]{1,0:T(8,128)(2,1)} async-done(((bf16[2048,256]{1,0:T(8,128)(2,1)}), bf16[2048,1024]{1,0:T(8,128)(2,1)}) %all-gather.7.cloned.1.call-update) | async-done | bytes 4194320 | tf_op jit(solution)/shard_map/all_gather | solution.py:65
  208.5 9.6 %multiply_convert_fusion.1 = (bf16[2048,1024]{1,0:T(8,128)(2,1)S(1)}, f32[2048,1024]{1,0:T(8,128)}) fusion(f32[1024]{0:T(1024)S(1)} %fusion.37, f32[1024]{0:T(1024)S(1)} %copy-done.38, bf16[2048,1024]{1,0:T(8,128)(2,1)} %all-gather.7.cloned.1.call-done, bf16[1024,1024]{1,0:T(8,128)(2,1)} %param.36), kind=kOutput, calls=%fused_computation.19 | convolution fusion | flops 4309647360 | bytes 18882560 | tf_op jit(solution)/shard_map/dot_general | solution.py:201
  220.1 6.0 convolution_convert_fusion.2
  226.2 44.5 %reduce-scatter.7.cloned.1.call-done = bf16[2048,256]{1,0:T(8,128)(2,1)} async-done(((bf16[2048,1024]{1,0:T(8,128)(2,1)}), bf16[2048,256]{1,0:T(8,128)(2,1)}) %reduce-scatter.7.cloned.1.call-update) | async-done | bytes 1048592 | tf_op jit(solution)/shard_map/reduce_scatter | solution.py:69
  273.2 5.9 psum.191
  281.8 5.8 psum.192
  287.6 6.7 fusion.54
  294.3 10.6 %all-reduce.3 = (f32[2048]{0:T(1024)S(1)}, f32[2048]{0:T(1024)S(1)}) all-reduce(f32[2048]{0:T(1024)S(1)} %get-tuple-element.114, f32[2048]{0:T(1024)S(1)} %get-tuple-element.115), channel_id=1, replica_groups=mesh['dp'=8,'hid'=4] {'hid'}, use_global_device_ids=true, to_apply=%region_15.16 | all-reduce | flops 4096 | bytes 32768 | tf_op jit(solution)/shard_map/psum | solution.py:96
  304.9 5.9 multiply_convert_fusion.7
  310.9 35.9 %all-gather.9.cloned.1.call-done = bf16[2048,1024]{1,0:T(8,128)(2,1)} async-done(((bf16[2048,256]{1,0:T(8,128)(2,1)}), bf16[2048,1024]{1,0:T(8,128)(2,1)}) %all-gather.9.cloned.1.call-update) | async-done | bytes 4194320 | tf_op jit(solution)/shard_map/all_gather | solution.py:75
  346.8 12.4 %fusion.57 = (bf16[1024]{0:T(1024)(128)(2,1)S(1)}, bf16[2048,1024]{1,0:T(8,128)(2,1)S(1)}, f32[2048,1024]{1,0:T(8,128)}) fusion(f32[2048,1024]{1,0:T(8,128)} %get-tuple-element.167, f32[1024]{0:T(1024)S(1)} %copy-done.38, f32[1024]{0:T(1024)S(1)} %fusion.37, bf16[2048,1024]{1,0:T(8,128)(2,1)} %all-gather.9.cloned.1.call-done, ...), kind=kOutput, calls=%fused_computation.148 | convolution fusion | flops 4322229248 | bytes 27273216 | tf_op jit(solution)/shard_map/dot_general | solution.py:59
  361.2 6.3 convolution_convert_fusion.1
  367.6 44.5 %reduce-scatter.9.cloned.1.call-done = bf16[2048,256]{1,0:T(8,128)(2,1)} async-done(((bf16[2048,1024]{1,0:T(8,128)(2,1)}), bf16[2048,256]{1,0:T(8,128)(2,1)}) %reduce-scatter.9.cloned.1.call-update) | async-done | bytes 1048592 | tf_op jit(solution)/shard_map/reduce_scatter | solution.py:79
  412.1 3.4 multiply_reduce_fusion.6
  415.4 10.1 %all-reduce.2 = (f32[2048]{0:T(1024)S(1)}, f32[2048]{0:T(1024)S(1)}) all-reduce(f32[2048]{0:T(1024)S(1)} %get-tuple-element.111, f32[2048]{0:T(1024)S(1)} %get-tuple-element.117), channel_id=1, replica_groups=mesh['dp'=8,'hid'=4] {'hid'}, use_global_device_ids=true, to_apply=%region_20.21 | all-reduce | flops 4096 | bytes 32768 | tf_op jit(solution)/shard_map/psum | solution.py:96
  425.6 3.5 multiply_reduce_fusion.2
  434.4 9.5 %convolution_convert_fusion.4 = bf16[1024,1024]{1,0:T(8,128)(2,1)} fusion(bf16[2048,1024]{1,0:T(8,128)(2,1)} %copy-done.50, bf16[2048,1024]{1,0:T(8,128)(2,1)} %all-gather.9.cloned.1.call-done), kind=kOutput, calls=%fused_computation.64 | convolution fusion | flops 4296015872 | bytes 10485760 | tf_op jit(solution)/shard_map/dot_general | solution.py:53
  444.0 5.8 convolution_convert_fusion.5
  449.8 17.6 %all-gather.11.cloned.1.call-done = bf16[2048,1024]{1,0:T(8,128)(2,1)} async-done(((bf16[2048,256]{1,0:T(8,128)(2,1)}), bf16[2048,1024]{1,0:T(8,128)(2,1)}) %all-gather.11.cloned.1.call-update) | async-done | bytes 4194320 | tf_op jit(solution)/shard_map/all_gather | solution.py:75
  467.4 5.5 multiply_reduce_fusion.4
  472.9 5.1 reshape.157
  477.9 4.7 copy.119
  482.7 9.3 %fusion.62 = (bf16[4,64]{1,0:T(4,128)(2,1)S(1)}, bf16[4,512,4,64]{1,3,2,0:T(8,128)(2,1)S(1)}) fusion(f32[4,4,512,512]{2,3,1,0:T(8,128)} %get-tuple-element.165, f32[4,4,512]{2,1,0:T(4,128)S(1)} %bitcast.99, f32[4,512,4,64]{1,3,2,0:T(8,128)} %copy.119, f32[4]{0:T(128)S(1)} %get-tuple-element.155), kind=kOutput, calls=%fused_computation.152 | convolution fusion | flops 547356416 | bytes 19956240 | tf_op jit(solution)/shard_map/shqk,sqhd->skhd/dot_general | solution.py:263
  492.0 11.4 %multiply_reduce_fusion = (f32[4,4,512]{2,1,0:T(4,128)S(1)}, f32[4,4,512,512]{2,3,1,0:T(8,128)}) fusion(f32[4,4,512,512]{2,3,1,0:T(8,128)} %get-tuple-element.165, f32[4,4,512]{2,1,0:T(4,128)S(1)} %bitcast.100, bf16[4,512,4,64]{1,3,2,0:T(8,128)(2,1)S(1)} %copy-done.18, f32[4,512,4,64]{1,3,2,0:T(8,128)S(1)} %copy-done.7, f32[4]{0:T(128)S(1)} %get-tuple-element.155), kind=kOutput, calls=%fused_computation.1 | convolution fusion | flops 550494208 | bytes 36765712 | tf_op jit(solution)/shard_map/sqhd,skhd->shqk/dot_general | solution.py:241
  503.5 12.1 %multiply_convert_fusion = bf16[4,4,512,512]{2,3,1,0:T(8,128)(2,1)S(1)} fusion(f32[4,4,512,512]{2,3,1,0:T(8,128)} %get-tuple-element.170, f32[4,4,512,512]{2,3,1,0:T(8,128)} %get-tuple-element.165, f32[4,4,512]{2,1,0:T(4,128)S(1)} %get-tuple-element.169, f32[4,4,512]{2,1,0:T(4,128)S(1)} %bitcast.101), kind=kLoop, calls=%fused_computation | loop fusion | flops 16777216 | bytes 42008576 | tf_op jit(solution)/shard_map/convert_element_type | solution.py:245
  537.1 3.4 add_convert_fusion
  551.4 42.3 %psum.215 = f32[]{:T(128)} all-reduce(f32[]{:T(128)} %get-tuple-element.116), channel_id=1, replica_groups=mesh['dp'=8,'hid'=4] {'dp','hid'}, use_global_device_ids=true, to_apply=%region_59.60 | all-reduce | flops 1 | bytes 8 | tf_op jit(solution)/shard_map/psum | solution.py:212
  594.3 7.0 multiply_reduce_fusion.1
  601.8 23.1 %all-reduce.4 = (bf16[256]{0:T(256)(128)(2,1)S(1)}, bf16[256]{0:T(256)(128)(2,1)S(1)}, bf16[256]{0:T(256)(128)(2,1)S(1)}, bf16[256]{0:T(256)(128)(2,1)S(1)}, bf1...) all-reduce(bf16[256]{0:T(256)(128)(2,1)S(1)} %reduce_sum.283, ...), channel_id=1, replica_groups=mesh['dp'=8,'hid'=4] {'dp'}, use_global_device_ids=true, to_apply=%region_25.26 | all-reduce | flops 4356 | bytes 17424 | tf_op jit(solution)/shard_map/psum | solution.py:306
  631.9 113.6 %all-reduce.8.cloned.1.call-done = (bf16[1024,256]{0,1:T(8,128)(2,1)}, bf16[1024,256]{0,1:T(8,128)(2,1)}, bf16[1024,256]{0,1:T(8,128)(2,1)}, bf16[256,1024]{1,0:...) async-done(((bf16[1024,256]{0,1:T(8,128)(2,1)}, bf16[1024,256]{0,1:T(8,128)(2,1)}, bf16[1024,256]{0,1:T(8,128)(2,1)}, bf16[256,1024]{1,0:T(8,128)(2,1)}, ...) | async-done | bytes 6291472 | tf_op jit(solution)/shard_map/psum | solution.py:305
  752.4 2.8 convert_element_type.275
  757.7 33.6 %reduce-scatter.11.cloned.1.call-done = bf16[2048,256]{1,0:T(8,128)(2,1)} async-done(((bf16[2048,1024]{1,0:T(8,128)(2,1)}), bf16[2048,256]{1,0:T(8,128)(2,1)}) %reduce-scatter.11.cloned.1.call-update) | async-done | bytes 1048592 | tf_op jit(solution)/shard_map/reduce_scatter | solution.py:79
  791.4 3.4 convert_add_fusion
  (197 shorter events, 75.7 us)
Async XLA Ops:
  7.2 212.9 %copy-start = (bf16[1024,1024]{1,0:T(8,128)(2,1)S(1)}, bf16[1024,1024]{1,0:T(8,128)(2,1)}, u32[]{:S(2)}) copy-start(bf16[1024,1024]{1,0:T(8,128)(2,1)} %param.38) | copy-start | bytes 6291460
  7.2 40.1 %all-gather.5.cloned.1.call-start = ((), (), s32[]{:S(2)}) async-start(), calls=%async_computation.4 | async-start | bytes 5242880 | tf_op jit(solution)/shard_map/all_gather | solution.py:65
  7.9 146.6 %reduce-scatter.5.cloned.1.call-start = ((), (), s32[]{:S(2)}) async-start(), calls=%async_computation.5 | async-start | bytes 5242880 | tf_op jit(solution)/shard_map/reduce_scatter | solution.py:69
  52.7 4.1 copy-start.47
  62.1 2.9 copy-start.48
  65.1 13.4 %copy-start.9 = (bf16[4,512,4,64]{1,3,2,0:T(8,128)(2,1)}, bf16[4,512,4,64]{1,3,2,0:T(8,128)(2,1)S(1)}, u32[]{:S(2)}) copy-start(bf16[4,512,4,64]{1,3,2,0:T(8,128)(2,1)S(1)} %copy.113) | copy-start | bytes 3145732
  87.0 8.3 %copy-start.17 = (bf16[4,512,4,64]{1,3,2,0:T(8,128)(2,1)S(1)}, bf16[4,512,4,64]{1,3,2,0:T(8,128)(2,1)}, u32[]{:S(2)}) copy-start(bf16[4,512,4,64]{1,3,2,0:T(8,128)(2,1)} %copy.115) | copy-start | bytes 3145732
  109.9 44.6 %copy-start.2 = (bf16[2048,256]{1,0:T(8,128)(2,1)S(1)}, bf16[2048,256]{1,0:T(8,128)(2,1)}, u32[]{:S(2)}) copy-start(bf16[2048,256]{1,0:T(8,128)(2,1)} %param.26) | copy-start | bytes 3145732
  109.9 44.6 %copy-start.28 = (f32[256]{0:T(256)S(1)}, f32[256]{0:T(256)}, u32[]{:S(2)}) copy-start(f32[256]{0:T(256)} %param.33) | copy-start | bytes 3076
  109.9 98.6 %all-gather.7.cloned.1.call-start = ((), (), s32[]{:S(2)}) async-start(), calls=%async_computation.6 | async-start | bytes 5242880 | tf_op jit(solution)/shard_map/all_gather | solution.py:65
  154.5 15.4 %copy-start.30 = (f32[256]{0:T(256)S(1)}, f32[256]{0:T(256)}, u32[]{:S(2)}) copy-start(f32[256]{0:T(256)} %param.34) | copy-start | bytes 3076
  154.5 15.4 %copy-start.34 = (f32[256]{0:T(256)S(1)}, f32[256]{0:T(256)}, u32[]{:S(2)}) copy-start(f32[256]{0:T(256)} %param.35) | copy-start | bytes 3076
  170.0 2.7 copy-start.29
  170.0 2.7 copy-start.32
  170.0 38.5 %copy-start.38 = (f32[1024]{0:T(1024)S(1)}, f32[1024]{0:T(1024)}, u32[]{:S(2)}) copy-start(f32[1024]{0:T(1024)} %param.37) | copy-start | bytes 12292
  172.6 98.1 %reduce-scatter.7.cloned.1.call-start = ((), (), s32[]{:S(2)}) async-start(), calls=%async_computation.7 | async-start | bytes 5242880 | tf_op jit(solution)/shard_map/reduce_scatter | solution.py:69
  226.2 44.6 %copy-start.35 = (f32[256]{0:T(256)S(1)}, f32[256]{0:T(256)}, u32[]{:S(2)}) copy-start(f32[256]{0:T(256)} %param.39) | copy-start | bytes 3076
  226.2 120.6 %all-gather.9.cloned.1.call-start = ((), (), s32[]{:S(2)}) async-start(), calls=%async_computation.8 | async-start | bytes 5242880 | tf_op jit(solution)/shard_map/all_gather | solution.py:75
  273.2 14.4 %copy-start.39 = (f32[256]{0:T(256)S(1)}, f32[256]{0:T(256)}, u32[]{:S(2)}) copy-start(f32[256]{0:T(256)} %param.41) | copy-start | bytes 3076
  273.2 14.4 %copy-start.40 = (f32[256]{0:T(256)S(1)}, f32[256]{0:T(256)}, u32[]{:S(2)}) copy-start(f32[256]{0:T(256)} %param.40) | copy-start | bytes 3076
  310.8 101.2 %reduce-scatter.9.cloned.1.call-start = ((), (), s32[]{:S(2)}) async-start(), calls=%async_computation.9 | async-start | bytes 5242880 | tf_op jit(solution)/shard_map/reduce_scatter | solution.py:79
  346.8 14.4 %copy-start.46 = (bf16[1024,1024]{1,0:T(8,128)(2,1)S(1)}, bf16[1024,1024]{1,0:T(8,128)(2,1)}, u32[]{:S(2)}) copy-start(bf16[1024,1024]{1,0:T(8,128)(2,1)} %param.36) | copy-start | bytes 6291460
  367.5 44.6 %copy-start.3 = (bf16[2048,256]{1,0:T(8,128)(2,1)S(1)}, bf16[2048,256]{1,0:T(8,128)(2,1)}, u32[]{:S(2)}) copy-start(bf16[2048,256]{1,0:T(8,128)(2,1)} %reduce-scatter.5.cloned.1.call-done) | copy-start | bytes 3145732
  367.5 44.6 %copy-start.8 = (bf16[2048,256]{1,0:T(8,128)(2,1)S(1)}, bf16[2048,256]{1,0:T(8,128)(2,1)}, u32[]{:S(2)}) copy-start(bf16[2048,256]{1,0:T(8,128)(2,1)} %reduce-scatter.7.cloned.1.call-done) | copy-start | bytes 3145732
  367.5 99.9 %all-gather.11.cloned.1.call-start = ((), (), s32[]{:S(2)}) async-start(), calls=%async_computation.10 | async-start | bytes 5242880 | tf_op jit(solution)/shard_map/all_gather | solution.py:75
  431.7 313.8 %all-reduce.8.cloned.1.call-start = ((), (), s32[]{:S(2)}) async-start(), calls=%async_computation.12 | async-start | bytes 12582912 | tf_op jit(solution)/shard_map/psum | solution.py:305
  434.4 9.6 %copy-start.45 = (bf16[2048,1024]{1,0:T(8,128)(2,1)S(1)}, bf16[2048,1024]{1,0:T(8,128)(2,1)}, u32[]{:S(2)}) copy-start(bf16[2048,1024]{1,0:T(8,128)(2,1)} %all-gather.7.cloned.1.call-done) | copy-start | bytes 12582916
  434.4 9.6 %copy-start.52 = (bf16[2048,1024]{1,0:T(8,128)(2,1)S(1)}, bf16[2048,1024]{1,0:T(8,128)(2,1)}, u32[]{:S(2)}) copy-start(bf16[2048,1024]{1,0:T(8,128)(2,1)} %copy-done.51) | copy-start | bytes 12582916
  444.0 23.4 %copy-start.22 = (bf16[256,1024]{1,0:T(8,128)(2,1)S(1)}, bf16[256,1024]{1,0:T(8,128)(2,1)}, u32[]{:S(2)}) copy-start(bf16[256,1024]{1,0:T(8,128)(2,1)} %param.32) | copy-start | bytes 1572868
  482.7 9.3 %copy-start.7 = (f32[4,512,4,64]{1,3,2,0:T(8,128)S(1)}, f32[4,512,4,64]{1,3,2,0:T(8,128)}, u32[]{:S(2)}) copy-start(f32[4,512,4,64]{1,3,2,0:T(8,128)} %copy.119) | copy-start | bytes 6291460
  482.7 9.3 %copy-start.18 = (bf16[4,512,4,64]{1,3,2,0:T(8,128)(2,1)S(1)}, bf16[4,512,4,64]{1,3,2,0:T(8,128)(2,1)}, u32[]{:S(2)}) copy-start(bf16[4,512,4,64]{1,3,2,0:T(8,128)(2,1)} %copy.115) | copy-start | bytes 3145732
  503.5 12.1 %copy-start.10 = (bf16[4,512,4,64]{1,3,2,0:T(8,128)(2,1)S(1)}, bf16[4,512,4,64]{1,3,2,0:T(8,128)(2,1)}, u32[]{:S(2)}) copy-start(bf16[4,512,4,64]{1,3,2,0:T(8,128)(2,1)} %copy-done.9) | copy-start | bytes 3145732
  515.6 2.6 copy-start.11
  520.9 5.4 copy-start.15
  524.2 6.9 copy-start.13
  524.2 2.8 copy-start.44
  533.1 2.6 copy-start.24
  533.1 258.3 %reduce-scatter.11.cloned.1.call-start = ((), (), s32[]{:S(2)}) async-start(), calls=%async_computation.11 | async-start | bytes 5242880 | tf_op jit(solution)/shard_map/reduce_scatter | solution.py:79
  540.5 3.2 copy-start.42
  540.5 5.7 copy-start.31
  594.3 7.1 copy-start.33
  594.3 7.1 copy-start.37
  594.3 7.5 copy-start.43
  745.5 4.7 copy-start.27
  745.5 5.9 copy-start.26
  747.8 4.6 copy-start.20
  752.4 2.8 copy-start.19
  755.2 39.5 %copy-start.1 = (bf16[1024,1024]{1,0:T(8,128)(2,1)S(1)}, bf16[1024,1024]{1,0:T(8,128)(2,1)}, u32[]{:S(2)}) copy-start(bf16[1024,1024]{1,0:T(8,128)(2,1)} %param.38) | copy-start | bytes 6291460
  (14 other events, 21.0 us)
Sparse Core Ops, SparseCore 0:
  9.6 37.7 all-gather.4
  110.0 44.4 reduce-scatter.4
  172.7 35.7 all-gather.6
  226.3 44.3 reduce-scatter.6
  311.0 35.7 all-gather.8
  367.6 44.3 reduce-scatter.8
  431.8 35.5 all-gather.10
  533.2 212.1 all-reduce.7
  748.0 43.3 reduce-scatter.10
where the time goes:
time: 813 us; the launch traced here: 803 us
  waiting for transfers between devices  406 us (50%)
  matrix products  126 us (15%)
  blocking collectives  109 us (13%)
  other arithmetic  82.2 us (10%)
  local copies, waits for them, and re-layouts  55.4 us (7%)
  between operations  23.3 us (3%)
    psum x1, waiting for transfers between devices, on_device(): lax.psum(query_weight_grad.astype(jnp.bfloat16), 'dp').astype(jnp.float32)  114 us
    reduce_scatter x2, waiting for transfers between devices, branch_total(): lax.psum_scatter(partial_sum.astype(jnp.bfloat16), 'hid', scatter_dimensi...  87.1 us
    reduce_scatter x2, waiting for transfers between devices, input_total(): lax.psum_scatter(partial_sum.astype(jnp.bfloat16), 'hid', scatter_dimensi...  78.2 us
    all_gather x2, waiting for transfers between devices, gather_features(): return lax.all_gather(sharded, 'hid', axis=1, tiled=True)  72.9 us
    all_gather x2, waiting for transfers between devices, gather_grads(): return lax.all_gather(sharded, 'hid', axis=1, tiled=True)  53.5 us
    psum x1, blocking collectives, on_device(): squared = lax.psum(jnp.sum(live_rows * differ * differ), ('dp', 'hid'))  42.3 us
    dot_general x6, matrix products, times_transpose(): lax.dot_general(left_side, right_side, (((1,), (1,)), ((), ())), preferre...  30.1 us
    dot_general x6, matrix products, inner_rows(): lax.dot_general(left_side, right_side, (((0,), (0,)), ((), ())), preferre...  23.6 us
  transfers between devices with their start and end apart: 9, of which 9 were waited for; matrix products, arithmetic and copies ran while one was open for 7% of the time, Pallas kernels for 0%

commit v1 on v0

--- a/solution.py
+++ b/solution.py
@@ -18,6 +18,27 @@
 ROOT_TWO_PI = 2.5066282746310002
 
 
+def gather_around(x, axis, dim):
+    count, mine, extent = (lax.axis_size(axis), lax.axis_index(axis), x.shape[dim])
+    ahead = [(i, (i + 1) % count) for i in range(count)]
+    left = [(i, (i - 1) % count) for i in range(count)]
+    out = jnp.zeros((*x.shape[:dim], count * extent, *x.shape[dim + 1 :]), x.dtype)
+    out = lax.dynamic_update_slice_in_dim(out, x, mine * extent, axis=dim)
+    from_left = from_right = x
+    half = count // 2
+    for turn in range(1, half + 1):
+        from_left = lax.ppermute(from_left, axis, ahead)
+        out = lax.dynamic_update_slice_in_dim(
+            out, from_left, (mine - turn) % count * extent, axis=dim
+        )
+        if turn < count - half:
+            from_right = lax.ppermute(from_right, axis, left)
+            out = lax.dynamic_update_slice_in_dim(
+                out, from_right, (mine + turn) % count * extent, axis=dim
+            )
+    return out
+
+
 def erf_gelu(values):
     return 0.5 * values * (1.0 + lax.erf(values * ROOT_HALF))
 
@@ -62,7 +83,7 @@
 
 
 def gather_features(sharded):
-    return lax.all_gather(sharded, "hid", axis=1, tiled=True)
+    return gather_around(sharded, "hid", 1)
 
 
 def branch_total(partial_sum):

time: 813 us -> 827 us (1.017)
  local copies, waits for them, and re-layouts: 55.4 us -> 73.7 us
  waiting for transfers between devices: 406 us -> 396 us
    all_gather x2 -> x0, waiting for transfers between devices: 72.9 us -> none  [gather_features(): return lax.all_gather(sharded, 'hid', axis=1, tiled=True)]
    ppermute x0 -> x6, waiting for transfers between devices: none -> 57.7 us  [the longest x4 57.7 us: gather_around(): from_left = lax.ppermute(from_left, axis, ahead)]
    dynamic_update_slice x0 -> x7, local copies, waits for them, and re-layouts: none -> 11.2 us  [the longest x4 7.26 us: gather_around(): lax.dynamic_update_slice_in_dim(out, from_left, (mine - turn) % count * e...]
    unnamed x114 -> x123, local copies, waits for them, and re-layouts: 19 us -> 18.4 us
  transfers between devices with their start and end apart: 9 -> 13, of which waited for: 9 -> 11; matrix products, arithmetic and copies ran while one was open for 7% -> 8% of each run, Pallas kernels for 0% -> 0%
where the time goes in v1:
time: 827 us; the launch traced here: 823 us
  waiting for transfers between devices  396 us (48%)
  matrix products  125 us (15%)
  blocking collectives  109 us (13%)
  other arithmetic  86.7 us (10%)
  local copies, waits for them, and re-layouts  73.7 us (9%)
  between operations  23.4 us (3%)
  starting transfers between devices  8.47 us (1%)
    psum x1, waiting for transfers between devices, on_device(): lax.psum(query_weight_grad.astype(jnp.bfloat16), 'dp').astype(jnp.float32)  114 us
    reduce_scatter x2, waiting for transfers between devices, branch_total(): lax.psum_scatter(partial_sum.astype(jnp.bfloat16), 'hid', scatter_dimensi...  92.2 us
    reduce_scatter x2, waiting for transfers between devices, input_total(): lax.psum_scatter(partial_sum.astype(jnp.bfloat16), 'hid', scatter_dimensi...  78.7 us
    ppermute x4, waiting for transfers between devices, gather_around(): from_left = lax.ppermute(from_left, axis, ahead)  57.7 us
    all_gather x2, waiting for transfers between devices, gather_grads(): return lax.all_gather(sharded, 'hid', axis=1, tiled=True)  53.7 us
    psum x1, blocking collectives, on_device(): squared = lax.psum(jnp.sum(live_rows * differ * differ), ('dp', 'hid'))  42.3 us
    dot_general x6, matrix products, times_transpose(): lax.dot_general(left_side, right_side, (((1,), (1,)), ((), ())), preferre...  30.2 us
    dot_general x6, matrix products, inner_rows(): lax.dot_general(left_side, right_side, (((0,), (0,)), ((), ())), preferre...  23.9 us
  transfers between devices with their start and end apart: 13, of which 11 were waited for; matrix products, arithmetic and copies ran while one was open for 8% of the time, Pallas kernels for 0%

profile of v1, /device:TPU:0, one launch (start us, length us, event | category | flops | bytes accessed | tf_op | source)
XLA Modules:
  0.0 822.8 jit_solution(14571504317886829301)
XLA Ops:
  9.8 21.4 %collective-permute-done = bf16[2048,256]{1,0:T(8,128)(2,1)} collective-permute-done((bf16[2048,256]{1,0:T(8,128)(2,1)}, bf16[2048,256]{1,0:T(8,128)(2,1)}, u32[]{:S(2)}, u32[]{:S(2)}) %collective-permute-start) | collective-permute-done | bytes 1048608 | tf_op jit(solution)/shard_map/ppermute | solution.py:30
  40.0 5.7 collective-permute-done.2
  51.3 4.9 reshape.160
  56.2 4.0 copy.105
  60.3 4.5 fusion.13
  64.8 4.4 reshape.159
  69.2 4.0 copy.104
  73.3 4.5 fusion.12
  77.8 4.4 reshape.158
  82.2 4.0 copy.106
  86.3 9.0 %fusion.58 = (f32[4,4,512]{2,1,0:T(4,128)S(1)}, f32[4,4,512,512]{2,3,1,0:T(8,128)}) fusion(bf16[4,512,4,64]{1,3,2,0:T(8,128)(2,1)} %copy.104, bf16[4,512,4,64]{1,3,2,0:T(8,128)(2,1)} %copy.105, pred[4,512]{1,0:T(4,128)(4,1)S(1)} %get-tuple-element.76), kind=kOutput, calls=%fused_computation.155 | convolution fusion | flops 549445632 | bytes 18909184 | tf_op jit(solution)/shard_map/sqhd,skhd->shqk/dot_general | solution.py:193
  95.2 8.3 %fusion = f32[4,4,512]{2,1,0:T(4,128)S(1)} fusion(f32[4,4,512,512]{2,3,1,0:T(8,128)} %get-tuple-element.79, f32[4,4,512]{2,1,0:T(4,128)S(1)} %get-tuple-element.78), kind=kLoop, calls=%fused_computation.6 | loop fusion | flops 8380416 | bytes 16842752 | tf_op jit(solution)/shard_map/reduce_sum | solution.py:201
  103.5 7.5 fusion.17
  114.6 3.4 convolution_convert_fusion
  120.0 46.4 %reduce-scatter.5.cloned.1.call-done = bf16[2048,256]{1,0:T(8,128)(2,1)} async-done(((bf16[2048,1024]{1,0:T(8,128)(2,1)}), bf16[2048,256]{1,0:T(8,128)(2,1)}) %reduce-scatter.5.cloned.1.call-update) | async-done | bytes 1048592 | tf_op jit(solution)/shard_map/reduce_scatter | solution.py:90
  168.1 5.9 psum.189
  176.0 5.8 psum.190
  188.3 22.1 %collective-permute-done.3 = bf16[2048,256]{1,0:T(8,128)(2,1)} collective-permute-done((bf16[2048,256]{1,0:T(8,128)(2,1)}, bf16[2048,256]{1,0:T(8,128)(2,1)}, u32[]{:S(2)}, u32[]{:S(2)}) %collective-permute-start.3) | collective-permute-done | bytes 1048608 | tf_op jit(solution)/shard_map/ppermute | solution.py:30
  216.4 8.6 %collective-permute-done.5 = bf16[2048,256]{1,0:T(8,128)(2,1)} collective-permute-done((bf16[2048,256]{1,0:T(8,128)(2,1)}, bf16[2048,256]{1,0:T(8,128)(2,1)}, u32[]{:S(2)}, u32[]{:S(2)}) %collective-permute-start.5) | collective-permute-done | bytes 1048608 | tf_op jit(solution)/shard_map/ppermute | solution.py:30
  227.2 9.1 %multiply_convert_fusion.1 = (bf16[2048,1024]{1,0:T(8,128)(2,1)S(1)}, f32[2048,1024]{1,0:T(8,128)}) fusion(f32[1024]{0:T(1024)S(1)} %fusion.34, f32[1024]{0:T(1024)S(1)} %copy-done.44, bf16[2048,1024]{1,0:T(8,128)(2,1)} %constant_dynamic-update-slice_fusion, bf16[1024,1024]{1,0:T(8,128)(2,1)S(1)} %copy-done.51), kind=kOutput, calls=%fused_computation.19 | convolution fusion | flops 4309647360 | bytes 18882560 | tf_op jit(solution)/shard_map/dot_general | solution.py:222
  238.2 6.0 convolution_convert_fusion.2
  244.6 45.8 %reduce-scatter.7.cloned.1.call-done = bf16[2048,256]{1,0:T(8,128)(2,1)} async-done(((bf16[2048,1024]{1,0:T(8,128)(2,1)}), bf16[2048,256]{1,0:T(8,128)(2,1)}) %reduce-scatter.7.cloned.1.call-update) | async-done | bytes 1048592 | tf_op jit(solution)/shard_map/reduce_scatter | solution.py:90
  292.8 5.9 psum.191
  301.4 5.8 psum.192
  307.2 6.3 fusion.51
  313.5 10.6 %all-reduce.3 = (f32[2048]{0:T(1024)S(1)}, f32[2048]{0:T(1024)S(1)}) all-reduce(f32[2048]{0:T(1024)S(1)} %get-tuple-element.26, f32[2048]{0:T(1024)S(1)} %get-tuple-element.27), channel_id=1, replica_groups=mesh['dp'=8,'hid'=4] {'hid'}, use_global_device_ids=true, to_apply=%region_15.16 | all-reduce | flops 4096 | bytes 32768 | tf_op jit(solution)/shard_map/psum | solution.py:117
  324.1 5.9 multiply_convert_fusion.7
  330.1 35.9 %all-gather.3.cloned.1.call-done = bf16[2048,1024]{1,0:T(8,128)(2,1)} async-done(((bf16[2048,256]{1,0:T(8,128)(2,1)}), bf16[2048,1024]{1,0:T(8,128)(2,1)}) %all-gather.3.cloned.1.call-update) | async-done | bytes 4194320 | tf_op jit(solution)/shard_map/all_gather | solution.py:96
  366.0 12.4 %fusion.54 = (bf16[1024]{0:T(1024)(128)(2,1)S(1)}, bf16[2048,1024]{1,0:T(8,128)(2,1)S(1)}, f32[2048,1024]{1,0:T(8,128)}) fusion(f32[2048,1024]{1,0:T(8,128)} %get-tuple-element.81, f32[1024]{0:T(1024)S(1)} %copy-done.44, f32[1024]{0:T(1024)S(1)} %fusion.34, bf16[2048,1024]{1,0:T(8,128)(2,1)} %all-gather.3.cloned.1.call-done, bf16[1024,1024]{1,0:T(8,128)(2,1)S(1)} %copy-done), kind=kOutput, calls=%fused_computation.153 | convolution fusion | flops 4322229248 | bytes 27273216 | tf_op jit(solution)/shard_map/dot_general | solution.py:80
  380.4 6.3 convolution_convert_fusion.1
  386.8 44.5 %reduce-scatter.9.cloned.1.call-done = bf16[2048,256]{1,0:T(8,128)(2,1)} async-done(((bf16[2048,1024]{1,0:T(8,128)(2,1)}), bf16[2048,256]{1,0:T(8,128)(2,1)}) %reduce-scatter.9.cloned.1.call-update) | async-done | bytes 1048592 | tf_op jit(solution)/shard_map/reduce_scatter | solution.py:100
  434.7 10.1 %all-reduce.2 = (f32[2048]{0:T(1024)S(1)}, f32[2048]{0:T(1024)S(1)}) all-reduce(f32[2048]{0:T(1024)S(1)} %get-tuple-element.23, f32[2048]{0:T(1024)S(1)} %get-tuple-element.29), channel_id=1, replica_groups=mesh['dp'=8,'hid'=4] {'hid'}, use_global_device_ids=true, to_apply=%region_20.21 | all-reduce | flops 4096 | bytes 32768 | tf_op jit(solution)/shard_map/psum | solution.py:117
  444.8 3.5 multiply_reduce_fusion.2
  453.5 9.5 %convolution_convert_fusion.5 = bf16[1024,1024]{1,0:T(8,128)(2,1)} fusion(bf16[2048,1024]{1,0:T(8,128)(2,1)} %constant_dynamic-update-slice_fusion, bf16[2048,1024]{1,0:T(8,128)(2,1)} %copy-done.58), kind=kOutput, calls=%fused_computation.65 | convolution fusion | flops 4296015872 | bytes 10485760 | tf_op jit(solution)/shard_map/dot_general | solution.py:74
  463.0 5.8 convolution_convert_fusion.4
  468.9 17.8 %all-gather.5.cloned.1.call-done = bf16[2048,1024]{1,0:T(8,128)(2,1)} async-done(((bf16[2048,256]{1,0:T(8,128)(2,1)}), bf16[2048,1024]{1,0:T(8,128)(2,1)}) %all-gather.5.cloned.1.call-update) | async-done | bytes 4194320 | tf_op jit(solution)/shard_map/all_gather | solution.py:96
  486.7 5.5 multiply_reduce_fusion.4
  492.2 5.1 reshape.157
  497.2 4.8 copy.110
  502.0 9.3 %fusion.60 = (bf16[4,64]{1,0:T(4,128)(2,1)S(1)}, bf16[4,512,4,64]{1,3,2,0:T(8,128)(2,1)S(1)}) fusion(f32[4,4,512,512]{2,3,1,0:T(8,128)} %get-tuple-element.79, f32[4,4,512]{2,1,0:T(4,128)S(1)} %bitcast.93, f32[4,512,4,64]{1,3,2,0:T(8,128)} %copy.110, f32[4]{0:T(128)S(1)} %copy-done.41), kind=kOutput, calls=%fused_computation.157 | convolution fusion | flops 547356416 | bytes 19956240 | tf_op jit(solution)/shard_map/shqk,sqhd->skhd/dot_general | solution.py:284
  511.4 11.4 %multiply_reduce_fusion = (f32[4,4,512]{2,1,0:T(4,128)S(1)}, f32[4,4,512,512]{2,3,1,0:T(8,128)}) fusion(f32[4,4,512,512]{2,3,1,0:T(8,128)} %get-tuple-element.79, f32[4,4,512]{2,1,0:T(4,128)S(1)} %bitcast.94, bf16[4,512,4,64]{1,3,2,0:T(8,128)(2,1)S(1)} %copy-done.21, f32[4,512,4,64]{1,3,2,0:T(8,128)S(1)} %copy-done.8, f32[4]{0:T(128)S(1)} %copy-done.41), kind=kOutput, calls=%fused_computation.1 | convolution fusion | flops 550494208 | bytes 36765712 | tf_op jit(solution)/shard_map/sqhd,skhd->shqk/dot_general | solution.py:262
  522.7 12.1 %multiply_convert_fusion = bf16[4,4,512,512]{2,3,1,0:T(8,128)(2,1)S(1)} fusion(f32[4,4,512,512]{2,3,1,0:T(8,128)} %get-tuple-element.84, f32[4,4,512,512]{2,3,1,0:T(8,128)} %get-tuple-element.79, f32[4,4,512]{2,1,0:T(4,128)S(1)} %get-tuple-element.83, f32[4,4,512]{2,1,0:T(4,128)S(1)} %bitcast.95), kind=kLoop, calls=%fused_computation | loop fusion | flops 16777216 | bytes 42008576 | tf_op jit(solution)/shard_map/convert_element_type | solution.py:266
  557.0 3.4 add_convert_fusion
  571.2 42.3 %psum.215 = f32[]{:T(128)} all-reduce(f32[]{:T(128)} %get-tuple-element.28), channel_id=1, replica_groups=mesh['dp'=8,'hid'=4] {'dp','hid'}, use_global_device_ids=true, to_apply=%region_59.60 | all-reduce | flops 1 | bytes 8 | tf_op jit(solution)/shard_map/psum | solution.py:233
  614.2 7.0 multiply_reduce_fusion.1
  621.7 23.1 %all-reduce.4 = (bf16[256]{0:T(256)(128)(2,1)S(1)}, bf16[256]{0:T(256)(128)(2,1)S(1)}, bf16[256]{0:T(256)(128)(2,1)S(1)}, bf16[256]{0:T(256)(128)(2,1)S(1)}, bf1...) all-reduce(bf16[256]{0:T(256)(128)(2,1)S(1)} %reduce_sum.283, ...), channel_id=1, replica_groups=mesh['dp'=8,'hid'=4] {'dp'}, use_global_device_ids=true, to_apply=%region_25.26 | all-reduce | flops 4356 | bytes 17424 | tf_op jit(solution)/shard_map/psum | solution.py:327
  651.8 113.6 %all-reduce.8.cloned.1.call-done = (bf16[1024,256]{1,0:T(8,128)(2,1)}, bf16[1024,256]{1,0:T(8,128)(2,1)}, bf16[1024,256]{1,0:T(8,128)(2,1)}, bf16[256,1024]{1,0:...) async-done(((bf16[1024,256]{1,0:T(8,128)(2,1)}, bf16[1024,256]{1,0:T(8,128)(2,1)}, bf16[1024,256]{1,0:T(8,128)(2,1)}, bf16[256,1024]{1,0:T(8,128)(2,1)}, ...) | async-done | bytes 6291472 | tf_op jit(solution)/shard_map/psum | solution.py:326
  777.1 34.2 %reduce-scatter.11.cloned.1.call-done = bf16[2048,256]{1,0:T(8,128)(2,1)} async-done(((bf16[2048,1024]{1,0:T(8,128)(2,1)}), bf16[2048,256]{1,0:T(8,128)(2,1)}) %reduce-scatter.11.cloned.1.call-update) | async-done | bytes 1048592 | tf_op jit(solution)/shard_map/reduce_scatter | solution.py:100
  (224 shorter events, 107.7 us)
Async XLA Ops:
  7.2 231.0 %copy-start = (bf16[1024,1024]{1,0:T(8,128)(2,1)S(1)}, bf16[1024,1024]{1,0:T(8,128)(2,1)}, u32[]{:S(2)}) copy-start(bf16[1024,1024]{1,0:T(8,128)(2,1)} %param.38) | copy-start | bytes 6291460
  7.2 159.2 %reduce-scatter.5.cloned.1.call-start = ((), (), s32[]{:S(2)}) async-start(), calls=%async_computation.4 | async-start | bytes 5242880 | tf_op jit(solution)/shard_map/reduce_scatter | solution.py:90
  7.3 23.9 %collective-permute-start = (bf16[2048,256]{1,0:T(8,128)(2,1)}, bf16[2048,256]{1,0:T(8,128)(2,1)}, u32[]{:S(2)}, u32[]{:S(2)}) collective-permute-start(bf16[2048,256]{1,0:T(8,128)(2,1)} %param.26), channel_id=1, source_target_pairs={{0,1},{1,2},{2,3},{3,0},{4,5},{5,6},{6,7},{7,4},{8,9},{9,10},{10,1... | collective-permute-start | bytes 3145736 | tf_op jit(solution)/shard_map/ppermute | solution.py:30
  7.8 30.8 %collective-permute-start.1 = (bf16[2048,256]{1,0:T(8,128)(2,1)}, bf16[2048,256]{1,0:T(8,128)(2,1)}, u32[]{:S(2)}, u32[]{:S(2)}) collective-permute-start(bf16[2048,256]{1,0:T(8,128)(2,1)} %param.26), channel_id=1, source_target_pairs={{0,3},{1,0},{2,1},{3,2},{4,7},{5,4},{6,5},{7,6},{8,11},{9,8},{10,9... | collective-permute-start | bytes 3145736 | tf_op jit(solution)/shard_map/ppermute | solution.py:35
  31.2 14.5 %collective-permute-start.2 = (bf16[2048,256]{1,0:T(8,128)(2,1)}, bf16[2048,256]{1,0:T(8,128)(2,1)}, u32[]{:S(2)}, u32[]{:S(2)}) collective-permute-start(bf16[2048,256]{1,0:T(8,128)(2,1)} %collective-permute-done), channel_id=1, source_target_pairs={{0,1},{1,2},{2,3},{3,0},{4,5},{5,6},{6,7},{7,4},{8,9},{9,10},{10,1... | collective-permute-start | bytes 3145736 | tf_op jit(solution)/shard_map/ppermute | solution.py:30
  38.6 10.5 %copy-start.27 = (bf16[1024,256]{1,0:T(8,128)(2,1)S(1)}, bf16[1024,256]{1,0:T(8,128)(2,1)}, u32[]{:S(2)}) copy-start(bf16[1024,256]{1,0:T(8,128)(2,1)} %param.29) | copy-start | bytes 1572868
  56.2 4.1 copy-start.53
  69.2 4.1 copy-start.54
  95.2 8.3 %copy-start.20 = (bf16[4,512,4,64]{1,3,2,0:T(8,128)(2,1)S(1)}, bf16[4,512,4,64]{1,3,2,0:T(8,128)(2,1)}, u32[]{:S(2)}) copy-start(bf16[4,512,4,64]{1,3,2,0:T(8,128)(2,1)} %copy.106) | copy-start | bytes 3145732
  118.0 48.4 %copy-start.32 = (f32[256]{0:T(256)S(1)}, f32[256]{0:T(256)}, u32[]{:S(2)}) copy-start(f32[256]{0:T(256)} %param.33) | copy-start | bytes 3076
  118.0 172.3 %reduce-scatter.7.cloned.1.call-start = ((), (), s32[]{:S(2)}) async-start(), calls=%async_computation.5 | async-start | bytes 5242880 | tf_op jit(solution)/shard_map/reduce_scatter | solution.py:90
  183.0 27.9 %copy-start.36 = (f32[1024]{0:T(1024)S(1)}, f32[1024]{0:T(1024)}, u32[]{:S(2)}) copy-start(f32[1024]{0:T(1024)} %param.47) | copy-start | bytes 12292
  186.6 23.8 %collective-permute-start.3 = (bf16[2048,256]{1,0:T(8,128)(2,1)}, bf16[2048,256]{1,0:T(8,128)(2,1)}, u32[]{:S(2)}, u32[]{:S(2)}) collective-permute-start(bf16[2048,256]{1,0:T(8,128)(2,1)} %get-tuple-element.68), channel_id=1, source_target_pairs={{0,1},{1,2},{2,3},{3,0},{4,5},{5,6},{6,7},{7,4},{8,9},{9,10},{10,1... | collective-permute-start | bytes 3145736 | tf_op jit(solution)/shard_map/ppermute | solution.py:30
  186.6 27.4 %collective-permute-start.4 = (bf16[2048,256]{1,0:T(8,128)(2,1)}, bf16[2048,256]{1,0:T(8,128)(2,1)}, u32[]{:S(2)}, u32[]{:S(2)}) collective-permute-start(bf16[2048,256]{1,0:T(8,128)(2,1)} %get-tuple-element.68), channel_id=1, source_target_pairs={{0,3},{1,0},{2,1},{3,2},{4,7},{5,4},{6,5},{7,6},{8,11},{9,8},{10,9... | collective-permute-start | bytes 3145736 | tf_op jit(solution)/shard_map/ppermute | solution.py:35
  210.4 14.5 %collective-permute-start.5 = (bf16[2048,256]{1,0:T(8,128)(2,1)}, bf16[2048,256]{1,0:T(8,128)(2,1)}, u32[]{:S(2)}, u32[]{:S(2)}) collective-permute-start(bf16[2048,256]{1,0:T(8,128)(2,1)} %collective-permute-done.3), channel_id=1, source_target_pairs={{0,1},{1,2},{2,3},{3,0},{4,5},{5,6},{6,7},{7,4},{8,9},{9,10},{10,1... | collective-permute-start | bytes 3145736 | tf_op jit(solution)/shard_map/ppermute | solution.py:30
  214.0 13.2 %copy-start.44 = (f32[1024]{0:T(1024)S(1)}, f32[1024]{0:T(1024)}, u32[]{:S(2)}) copy-start(f32[1024]{0:T(1024)} %param.37) | copy-start | bytes 12292
  214.0 13.3 %copy-start.51 = (bf16[1024,1024]{1,0:T(8,128)(2,1)S(1)}, bf16[1024,1024]{1,0:T(8,128)(2,1)}, u32[]{:S(2)}) copy-start(bf16[1024,1024]{1,0:T(8,128)(2,1)} %param.36) | copy-start | bytes 6291460
  244.3 46.1 %copy-start.39 = (f32[256]{0:T(256)S(1)}, f32[256]{0:T(256)}, u32[]{:S(2)}) copy-start(f32[256]{0:T(256)} %param.39) | copy-start | bytes 3076
  244.3 121.7 %all-gather.3.cloned.1.call-start = ((), (), s32[]{:S(2)}) async-start(), calls=%async_computation.6 | async-start | bytes 5242880 | tf_op jit(solution)/shard_map/all_gather | solution.py:96
  292.8 14.4 %copy-start.45 = (f32[256]{0:T(256)S(1)}, f32[256]{0:T(256)}, u32[]{:S(2)}) copy-start(f32[256]{0:T(256)} %param.41) | copy-start | bytes 3076
  292.8 14.4 %copy-start.46 = (f32[256]{0:T(256)S(1)}, f32[256]{0:T(256)}, u32[]{:S(2)}) copy-start(f32[256]{0:T(256)} %param.40) | copy-start | bytes 3076
  330.1 101.2 %reduce-scatter.9.cloned.1.call-start = ((), (), s32[]{:S(2)}) async-start(), calls=%async_computation.7 | async-start | bytes 5242880 | tf_op jit(solution)/shard_map/reduce_scatter | solution.py:100
  366.0 14.3 %copy-start.52 = (bf16[1024,1024]{1,0:T(8,128)(2,1)S(1)}, bf16[1024,1024]{1,0:T(8,128)(2,1)}, u32[]{:S(2)}) copy-start(bf16[1024,1024]{1,0:T(8,128)(2,1)} %param.36) | copy-start | bytes 6291460
  386.7 44.6 %copy-start.4 = (bf16[2048,256]{1,0:T(8,128)(2,1)S(1)}, bf16[2048,256]{1,0:T(8,128)(2,1)}, u32[]{:S(2)}) copy-start(bf16[2048,256]{1,0:T(8,128)(2,1)} %reduce-scatter.5.cloned.1.call-done) | copy-start | bytes 3145732
  386.7 44.6 %copy-start.9 = (bf16[2048,256]{1,0:T(8,128)(2,1)S(1)}, bf16[2048,256]{1,0:T(8,128)(2,1)}, u32[]{:S(2)}) copy-start(bf16[2048,256]{1,0:T(8,128)(2,1)} %reduce-scatter.7.cloned.1.call-done) | copy-start | bytes 3145732
  386.7 99.9 %all-gather.5.cloned.1.call-start = ((), (), s32[]{:S(2)}) async-start(), calls=%async_computation.8 | async-start | bytes 5242880 | tf_op jit(solution)/shard_map/all_gather | solution.py:96
  450.9 314.4 %all-reduce.8.cloned.1.call-start = ((), (), s32[]{:S(2)}) async-start(), calls=%async_computation.10 | async-start | bytes 12582912 | tf_op jit(solution)/shard_map/psum | solution.py:326
  453.5 9.5 %copy-start.50 = (bf16[2048,1024]{1,0:T(8,128)(2,1)S(1)}, bf16[2048,1024]{1,0:T(8,128)(2,1)}, u32[]{:S(2)}) copy-start(bf16[2048,1024]{1,0:T(8,128)(2,1)} %all-gather.3.cloned.1.call-done) | copy-start | bytes 12582916
  453.5 9.5 %copy-start.57 = (bf16[2048,1024]{1,0:T(8,128)(2,1)S(1)}, bf16[2048,1024]{1,0:T(8,128)(2,1)}, u32[]{:S(2)}) copy-start(bf16[2048,1024]{1,0:T(8,128)(2,1)} %copy-done.56) | copy-start | bytes 12582916
  463.0 23.6 %copy-start.25 = (bf16[256,1024]{1,0:T(8,128)(2,1)S(1)}, bf16[256,1024]{1,0:T(8,128)(2,1)}, u32[]{:S(2)}) copy-start(bf16[256,1024]{1,0:T(8,128)(2,1)} %param.32) | copy-start | bytes 1572868
  497.2 4.8 copy-start.41
  502.0 9.3 %copy-start.8 = (f32[4,512,4,64]{1,3,2,0:T(8,128)S(1)}, f32[4,512,4,64]{1,3,2,0:T(8,128)}, u32[]{:S(2)}) copy-start(f32[4,512,4,64]{1,3,2,0:T(8,128)} %copy.110) | copy-start | bytes 6291460
  502.0 9.3 %copy-start.21 = (bf16[4,512,4,64]{1,3,2,0:T(8,128)(2,1)S(1)}, bf16[4,512,4,64]{1,3,2,0:T(8,128)(2,1)}, u32[]{:S(2)}) copy-start(bf16[4,512,4,64]{1,3,2,0:T(8,128)(2,1)} %copy.106) | copy-start | bytes 3145732
  522.7 12.1 %copy-start.10 = (bf16[4,512,4,64]{1,3,2,0:T(8,128)(2,1)S(1)}, bf16[4,512,4,64]{1,3,2,0:T(8,128)(2,1)}, u32[]{:S(2)}) copy-start(bf16[4,512,4,64]{1,3,2,0:T(8,128)(2,1)} %copy.104) | copy-start | bytes 3145732
  540.2 3.6 copy-start.15
  548.1 2.8 copy-start.12
  553.0 2.6 copy-start.28
  553.0 258.3 %reduce-scatter.11.cloned.1.call-start = ((), (), s32[]{:S(2)}) async-start(), calls=%async_computation.9 | async-start | bytes 5242880 | tf_op jit(solution)/shard_map/reduce_scatter | solution.py:100
  560.4 3.2 copy-start.48
  560.4 4.4 copy-start.33
  560.4 5.7 copy-start.35
  614.2 7.1 copy-start.37
  614.2 7.1 copy-start.43
  614.2 7.5 copy-start.49
  765.3 4.4 copy-start.31
  765.3 5.5 copy-start.30
  767.5 4.4 copy-start.23
  774.5 40.1 %copy-start.1 = (bf16[1024,1024]{1,0:T(8,128)(2,1)S(1)}, bf16[1024,1024]{1,0:T(8,128)(2,1)}, u32[]{:S(2)}) copy-start(bf16[1024,1024]{1,0:T(8,128)(2,1)} %param.38) | copy-start | bytes 6291460
  (24 other events, 38.3 us)
Sparse Core Ops, SparseCore 0:
  118.2 48.1 reduce-scatter.4
  244.4 45.9 reduce-scatter.6
  330.2 35.7 all-gather.2
  386.9 44.3 reduce-scatter.8
  451.0 35.5 all-gather.4
  553.1 212.1 all-reduce.7
  767.8 43.3 reduce-scatter.10
